TPU v7x, 512 devices: a whole 4x8x8 slice. The times are simulated.
512 devices in a mesh: imp: 32 (over z, x), adv: 16 (over y, core).
Axes of the slice: x: 4, y: 8, z: 8, core: 2. Of those that a mesh axis runs over, the one named last changes fastest.
Arguments:
- impression_vectors: bfloat16 [64, 65536], P(None, 'imp'), may hold values from -6 to 6
- advertiser_vectors: bfloat16 [64, 65536], P(None, ('imp', 'adv')), may hold values from -0.75 to 0.75
- spend_limits: float32 [65536], P(('imp', 'adv')), may hold values from 1024 to 8192
- capacity: float32 [65536], P('imp'), may hold values from 1024 to 8192
- blocks: int32 [512, 16, 8], P('imp', 'adv'), may hold values from 0 to 511, as said below
- counts: int32 [512, 16], P('imp', 'adv'), may hold values from 1 to 8, as said below
Outputs:
- prices: float32 [65536], P(('imp', 'adv'))
- impression_duals: float32 [65536], P('imp')
- impression_grad: bfloat16 [64, 65536], P(None, ('imp', 'adv'))
- advertiser_grad: bfloat16 [64, 65536], P(None, ('imp', 'adv'))
Inputs may be any that keep to these rules, and one draw needn't show every extreme that they name: Block numbers. Entry [g, a, k] names a block b with (b) % (the size of adv) == a. The 8 entries of one list are distinct; entries at slots k >= counts[g, a] are padding and name valid blocks too. `counts`: every group has one index of adv whose count is 8.
All inputs are finite; a program needn't handle non-finite values.
Results may differ from a plain program's by a relative error of at most 0.012.
Values may be sent and summed in bfloat16 or wider, within the bound.
No kernel may reach another device: no remote copies, remote signals or barrier semaphores. Data moves between devices by JAX's collectives and lax.ppermute only.
A program may use at most 64 MiB of HBM per device.

v0:
```python
import jax
import jax.numpy as jnp
from jax import lax
from jax.sharding import PartitionSpec as P

GROUP = 128
BLOCK = 128
ITERS = 3
BLK_DEV = 1


def local(impression_vectors, advertiser_vectors, spend_limits, capacity, blocks, counts):
    features = impression_vectors.shape[0]
    groups_here = blocks.shape[0]
    slot_count = blocks.shape[2]
    adv_devices = lax.axis_size("adv")
    block_ids = blocks.reshape(groups_here, slot_count)
    local_ids = block_ids // BLK_DEV // adv_devices * BLK_DEV + block_ids % BLK_DEV
    live_slots = (jnp.arange(slot_count)[None, :] < counts).astype(jnp.float32)
    viewers = impression_vectors.reshape(features, groups_here, GROUP)
    extent = slot_count * BLOCK
    own_count = spend_limits.shape[0]
    fetched = lax.all_gather(advertiser_vectors, "imp", axis=1, tiled=True)
    catalog = fetched.reshape(features, fetched.shape[1] // BLOCK, BLOCK)
    local_blocks = catalog.shape[1]

    def allocate(source, prices, duals, group_no):
        chosen = lax.dynamic_index_in_dim(local_ids, group_no, 0, keepdims=False)
        columns = jnp.take(source, chosen, axis=1).reshape(features, extent)
        viewer = lax.dynamic_index_in_dim(viewers, group_no, 1, keepdims=False)
        scores = lax.dot_general(
            viewer, columns, (((0,), (0,)), ((), ())), preferred_element_type=jnp.float32
        )
        charged = jnp.take(prices, chosen, axis=0).reshape(extent)
        shadow = lax.dynamic_slice_in_dim(duals, group_no * GROUP, GROUP)
        eligible = jnp.repeat(
            lax.dynamic_index_in_dim(live_slots, group_no, 0, keepdims=False), BLOCK
        )
        shares = jnp.clip(scores - charged[None, :] - shadow[:, None], 0.0, 1.0) * eligible[None, :]
        return (shares, chosen, columns, viewer)

    duals = jnp.zeros((groups_here * GROUP,), jnp.float32)
    range_prices = jnp.zeros((local_blocks, BLOCK), jnp.float32)
    own_prices = jnp.zeros((own_count,), jnp.float32)
    for iteration in range(ITERS):
        totals_prices = range_prices

        def advance(group_no, pair):
            outlay, demand = pair
            shares, chosen, _, _ = allocate(catalog, totals_prices, duals, group_no)
            outlay = outlay.at[chosen].add(jnp.sum(shares, axis=0).reshape(slot_count, BLOCK))
            demand = lax.dynamic_update_slice_in_dim(
                demand, jnp.sum(shares, axis=1), group_no * GROUP, 0
            )
            return (outlay, demand)

        totals_start = (
            jnp.zeros((local_blocks, BLOCK), jnp.float32),
            jnp.zeros((groups_here * GROUP,), jnp.float32),
        )
        outlay, demand = lax.fori_loop(0, groups_here, advance, totals_start)
        own_outlay = lax.psum_scatter(outlay.reshape(-1), "imp", scatter_dimension=0, tiled=True)
        dual_demand = demand
        dual_demand = lax.psum(dual_demand, "adv")
        duals = jnp.maximum(duals + dual_demand / capacity - 1.0, 0.0)
        own_prices = jnp.maximum(own_prices + own_outlay / spend_limits - 1.0, 0.0)
        range_prices = lax.all_gather(own_prices, "imp", axis=0, tiled=True).reshape(
            local_blocks, BLOCK
        )

    def grad_step(group_no, pair):
        imp_part, adv_part = pair
        shares, chosen, columns, viewer = allocate(catalog, range_prices, duals, group_no)
        weights = shares.astype(jnp.bfloat16)
        imp_cols = lax.dot_general(
            columns, weights, (((1,), (1,)), ((), ())), preferred_element_type=jnp.float32
        )
        imp_part = lax.dynamic_update_slice_in_dim(imp_part, imp_cols, group_no * GROUP, 1)
        adv_terms = jnp.dot(viewer, weights, preferred_element_type=jnp.float32).reshape(
            features, slot_count, BLOCK
        )
        adv_part = adv_part.at[:, chosen].add(adv_terms)
        return (imp_part, adv_part)

    start = (
        jnp.zeros((features, groups_here * GROUP), jnp.float32),
        jnp.zeros((features, local_blocks, BLOCK), jnp.float32),
    )
    imp_part, adv_part = lax.fori_loop(0, groups_here, grad_step, start)
    impression_grad = lax.psum_scatter(imp_part, "adv", scatter_dimension=1, tiled=True).astype(
        jnp.bfloat16
    )
    adv_rounded = (adv_part.reshape(features, -1) / GROUP).astype(jnp.bfloat16)
    advertiser_grad = (
        lax.psum_scatter(adv_rounded, "imp", scatter_dimension=1, tiled=True)
        .astype(jnp.float32)
        .astype(jnp.bfloat16)
    )
    return (own_prices, duals, impression_grad, advertiser_grad)


def solution(mesh):
    return jax.shard_map(
        local,
        mesh=mesh,
        in_specs=(
            P(None, "imp"),
            P(None, ("imp", "adv")),
            P(("imp", "adv")),
            P("imp"),
            P("imp", "adv", None),
            P("imp", "adv"),
        ),
        out_specs=(P(("imp", "adv")), P("imp"), P(None, ("imp", "adv")), P(None, ("imp", "adv"))),
        check_vma=False,
    )
```

profile of v0, /device:TPU:25, one launch (start us, length us, event | category | flops | bytes accessed | tf_op | source)
XLA Modules:
  0.0 1180.3 jit_solution(11911110707107156288)
XLA Ops:
  9.5 44.2 %all_gather.12 = bf16[64,4096]{1,0:T(8,128)(2,1)S(1)} all-gather(bf16[64,128]{1,0:T(8,128)(2,1)S(1)} %copy-done.7), channel_id=1, replica_groups=mesh['imp'=32,'adv'=16] {'imp'}, dimensions={1}, use_global_device_ids=true | all-gather | bytes 540672 | tf_op jit(solution)/shard_map/all_gather | solution.py:23
  53.8 41.5 %while.60 = (s32[]{:T(128)}, f32[32,128]{1,0:T(8,128)S(1)}, f32[2048]{0:T(1024)S(1)}, s32[16,8]{1,0:T(8,128)S(1)}, bf16[64,16,128]{2,0,1:T(8,128)(2,1)S(1)}, /*i...) while((s32[]{:T(128)}, f32[32,128]{1,0:T(8,128)S(1)}, ...), condition=%wide.region_4.7_spmd, body=%wide.region_0.6_spmd.sunk | while | flops 17500104 | bytes 485907 | solution.py:61
  95.4 35.8 %psum.21 = f32[2048]{0:T(1024)S(1)} all-reduce(f32[2048]{0:T(1024)S(1)} %get-tuple-element.597), channel_id=1, replica_groups=mesh['imp'=32,'adv'=16] {'adv'}, use_global_device_ids=true, to_apply=%region_6.9 | all-reduce | flops 2048 | bytes 16384 | tf_op jit(solution)/shard_map/psum | solution.py:64
  131.2 112.5 %all-reduce = f32[4096]{0:T(1024)S(1)} all-reduce(f32[4096]{0:T(1024)S(1)} %bitcast.255), channel_id=2, replica_groups=mesh['imp'=32,'adv'=16] {'imp'}, use_global_device_ids=true, to_apply=%region_5.8.clone | all-reduce | flops 4096 | bytes 32768
  243.8 1.3 dynamic-slice
  245.8 28.0 %all-gather = f32[32,1,128]{2,1,0:T(1,128)S(1)} all-gather(f32[1,1,128]{2,1,0:T(1,128)S(1)} %bitcast.260), channel_id=1, replica_groups=mesh['imp'=32,'adv'=16] {'imp'}, dimensions={0}, use_global_device_ids=true | all-gather | bytes 16896 | tf_op jit(solution)/shard_map/all_gather | solution.py:67
  273.8 42.5 %while.61 = (s32[]{:T(128)}, f32[32,128]{1,0:T(8,128)S(1)}, f32[2048]{0:T(1024)S(1)}, s32[16,8]{1,0:T(8,128)S(1)}, bf16[64,16,128]{2,0,1:T(8,128)(2,1)S(1)}, /*i...) while((s32[]{:T(128)}, f32[32,128]{1,0:T(8,128)S(1)}, ...), condition=%wide.region_11.14_spmd, body=%wide.region_7.13_spmd.sunk | while | flops 17631180 | bytes 471067 | solution.py:61
  316.3 58.5 %psum.22 = f32[2048]{0:T(1024)S(1)} all-reduce(f32[2048]{0:T(1024)S(1)} %get-tuple-element.599), channel_id=1, replica_groups=mesh['imp'=32,'adv'=16] {'adv'}, use_global_device_ids=true, to_apply=%region_13.16 | all-reduce | flops 2048 | bytes 16384 | tf_op jit(solution)/shard_map/psum | solution.py:64
  374.8 112.3 %all-reduce.1 = f32[4096]{0:T(1024)S(1)} all-reduce(f32[4096]{0:T(1024)S(1)} %bitcast.256), channel_id=3, replica_groups=mesh['imp'=32,'adv'=16] {'imp'}, use_global_device_ids=true, to_apply=%region_12.15.clone | all-reduce | flops 4096 | bytes 32768
  487.2 27.5 %all-gather.1 = f32[32,1,128]{2,1,0:T(1,128)S(1)} all-gather(f32[1,1,128]{2,1,0:T(1,128)S(1)} %bitcast.259), channel_id=1, replica_groups=mesh['imp'=32,'adv'=16] {'imp'}, dimensions={0}, use_global_device_ids=true | all-gather | bytes 16896 | tf_op jit(solution)/shard_map/all_gather | solution.py:67
  514.7 42.4 %while.62 = (s32[]{:T(128)}, f32[32,128]{1,0:T(8,128)S(1)}, f32[2048]{0:T(1024)S(1)}, s32[16,8]{1,0:T(8,128)S(1)}, bf16[64,16,128]{2,0,1:T(8,128)(2,1)S(1)}, /*i...) while((s32[]{:T(128)}, f32[32,128]{1,0:T(8,128)S(1)}, ...), condition=%wide.region_18.21_spmd, body=%wide.region_14.20_spmd.sunk | while | flops 17631180 | bytes 471067 | solution.py:61
  557.1 59.3 %psum.23 = f32[2048]{0:T(1024)S(1)} all-reduce(f32[2048]{0:T(1024)S(1)} %get-tuple-element.601), channel_id=1, replica_groups=mesh['imp'=32,'adv'=16] {'adv'}, use_global_device_ids=true, to_apply=%region_20.23 | all-reduce | flops 2048 | bytes 16384 | tf_op jit(solution)/shard_map/psum | solution.py:64
  617.1 111.9 %all-reduce.2 = f32[4096]{0:T(1024)S(1)} all-reduce(f32[4096]{0:T(1024)S(1)} %bitcast.257), channel_id=4, replica_groups=mesh['imp'=32,'adv'=16] {'imp'}, use_global_device_ids=true, to_apply=%region_19.22.clone | all-reduce | flops 4096 | bytes 32768
  729.6 27.5 %all-gather.2 = f32[32,1,128]{2,1,0:T(1,128)S(1)} all-gather(f32[1,1,128]{2,1,0:T(1,128)S(1)} %bitcast.261), channel_id=1, replica_groups=mesh['imp'=32,'adv'=16] {'imp'}, dimensions={0}, use_global_device_ids=true | all-gather | bytes 16896 | tf_op jit(solution)/shard_map/all_gather | solution.py:67
  757.2 95.1 %while.63 = (s32[]{:T(128)}, f32[64,2048]{1,0:T(8,128)S(1)}, f32[64,32,128]{2,0,1:T(8,128)S(1)}, s32[16,8]{1,0:T(8,128)S(1)}, bf16[64,32,128]{2,0,1:T(8,128)(2,1...) while((s32[]{:T(128)}, f32[64,2048]{1,0:T(8,128)S(1)}, ...), condition=%wide.region_23.26_spmd, body=%wide.region_21.25_spmd.sunk | while | flops 51185740 | bytes 2993603 | solution.py:89
  762.2 0.9 scatter_fusion
  768.2 0.9 scatter_fusion
  774.1 0.9 scatter_fusion
  780.0 0.9 scatter_fusion
  853.1 1.3 copy.68
  855.3 250.8 %reduce-scatter.7.cloned.1.call-done = bf16[128,64]{1,0:T(8,128)(2,1)} async-done(((bf16[4096,64]{1,0:T(8,128)(2,1)}), bf16[128,64]{1,0:T(8,128)(2,1)}) %reduce-scatter.7.cloned.1.call-update) | async-done | bytes 16400
  1106.1 1.4 copy.67
  1107.5 64.6 %reduce-scatter.5.cloned.1.call-done = f32[64,128]{1,0:T(8,128)} async-done(((f32[64,2048]{1,0:T(8,128)}), f32[64,128]{1,0:T(8,128)}) %reduce-scatter.5.cloned.1.call-update) | async-done | bytes 32784 | tf_op jit(solution)/shard_map/reduce_scatter | solution.py:90
  1172.1 1.4 convert_element_type.23
  (996 shorter events, 218.3 us)
Async XLA Ops:
  7.2 1.6 copy-start
  7.2 1098.9 %reduce-scatter.7.cloned.1.call-start = ((), (), s32[]{:S(2)}) async-start(), calls=%async_computation.3 | async-start | bytes 1081344
  245.8 28.0 %copy-start.2 = (f32[2048]{0:T(1024)S(1)}, f32[2048]{0:T(1024)}, u32[]{:S(2)}) copy-start(f32[2048]{0:T(1024)} %param.21) | copy-start | bytes 24580
  757.2 2.0 copy-start.5
  759.2 1.2 copy-start.3
  763.1 2.0 copy-start.5
  765.1 1.2 copy-start.3
  769.1 2.0 copy-start.5
  775.0 2.0 copy-start.5
  781.0 2.0 copy-start.5
  783.0 1.2 copy-start.3
  786.9 2.0 copy-start.5
  788.9 1.2 copy-start.3
  792.9 2.0 copy-start.5
  798.8 2.0 copy-start.5
  804.8 2.0 copy-start.5
  810.7 2.0 copy-start.5
  816.7 2.0 copy-start.5
  822.6 2.0 copy-start.5
  828.5 2.0 copy-start.5
  834.5 2.0 copy-start.5
  840.4 2.0 copy-start.5
  846.4 2.0 copy-start.5
  854.5 317.6 %reduce-scatter.5.cloned.1.call-start = ((), (), s32[]{:S(2)}) async-start(), calls=%async_computation.2 | async-start | bytes 557056 | tf_op jit(solution)/shard_map/reduce_scatter | solution.py:90
  (98 other events, 78.5 us)
Sparse Core Ops, SparseCore 0:
  854.6 251.3 reduce-scatter.6
  1108.8 63.2 reduce-scatter.4
where the time goes:
time: 1180 us
  blocking collectives  617 us (52%)
  waiting for transfers between devices  316 us (27%)
  local copies, waits for them, and re-layouts  133 us (11%)
  other arithmetic  62.3 us (5%)
  matrix products  30.7 us (3%)
  between operations  14.9 us (1%)
    unnamed x3, blocking collectives  337 us
    unnamed x3, waiting for transfers between devices  252 us
    psum x3, blocking collectives, local(): dual_demand = lax.psum(dual_demand, 'adv')  154 us
    all_gather x3, blocking collectives, local(): lax.all_gather(own_prices, 'imp', axis=0, tiled=True)  83 us
    reduce_scatter x1, waiting for transfers between devices, local(): lax.psum_scatter(imp_part, 'adv', scatter_dimension=1, tiled=True)  64.6 us
    all_gather x1, blocking collectives, local(): fetched = lax.all_gather(advertiser_vectors, 'imp', axis=1, tiled=True)  44.2 us
    gather x64, local copies, waits for them, and re-layouts, allocate(): columns = jnp.take(source, chosen, axis=1).reshape(features, extent)  36.6 us
    gather x64, local copies, waits for them, and re-layouts, allocate(): charged = jnp.take(prices, chosen, axis=0).reshape(extent)  35.6 us
  transfers between devices with their start and end apart: 2, of which 2 were waited for; matrix products, arithmetic and copies ran while one was open for 0% of the time, Pallas kernels for 0%

commit v1 on v0

--- a/solution.py
+++ b/solution.py
@@ -64,9 +64,9 @@
         dual_demand = lax.psum(dual_demand, "adv")
         duals = jnp.maximum(duals + dual_demand / capacity - 1.0, 0.0)
         own_prices = jnp.maximum(own_prices + own_outlay / spend_limits - 1.0, 0.0)
-        range_prices = lax.all_gather(own_prices, "imp", axis=0, tiled=True).reshape(
-            local_blocks, BLOCK
-        )
+        range_prices = jnp.concatenate(
+            lax.all_to_all(jnp.stack([own_prices] * lax.axis_size("imp")), "imp", 0, 0), axis=0
+        ).reshape(local_blocks, BLOCK)
 
     def grad_step(group_no, pair):
         imp_part, adv_part = pair

time: 1180 us -> 1110 us (0.941)
  blocking collectives: 617 us -> 524 us
  starting transfers between devices: 0.08 us -> 12.5 us
    all_gather x3 -> x0, blocking collectives: 83 us -> none  [local(): lax.all_gather(own_prices, 'imp', axis=0, tiled=True)]
    all_to_all x0 -> x3, waiting for transfers between devices: none -> 16.4 us  [local(): lax.all_to_all(jnp.stack([own_prices] * lax.axis_size('imp')), 'imp', 0, 0)]
    all_to_all x0 -> x3, starting transfers between devices: none -> 12.4 us  [local(): lax.all_to_all(jnp.stack([own_prices] * lax.axis_size('imp')), 'imp', 0, 0)]
    psum x3, blocking collectives: 154 us -> 141 us  [local(): dual_demand = lax.psum(dual_demand, 'adv')]
  transfers between devices with their start and end apart: 2 -> 5, of which waited for: 2 -> 4; matrix products, arithmetic and copies ran while one was open for 0% -> 0% of each run, Pallas kernels for 0% -> 0%
where the time goes in v1:
time: 1110 us
  blocking collectives  524 us (47%)
  waiting for transfers between devices  323 us (29%)
  local copies, waits for them, and re-layouts  135 us (12%)
  other arithmetic  62.3 us (6%)
  matrix products  30.7 us (3%)
  between operations  14.9 us (1%)
  starting transfers between devices  12.5 us (1%)
    unnamed x3, blocking collectives  339 us
    unnamed x3, waiting for transfers between devices  242 us
    psum x3, blocking collectives, local(): dual_demand = lax.psum(dual_demand, 'adv')  141 us
    reduce_scatter x1, waiting for transfers between devices, local(): lax.psum_scatter(imp_part, 'adv', scatter_dimension=1, tiled=True)  64.6 us
    all_gather x1, blocking collectives, local(): fetched = lax.all_gather(advertiser_vectors, 'imp', axis=1, tiled=True)  44.2 us
    gather x64, local copies, waits for them, and re-layouts, allocate(): columns = jnp.take(source, chosen, axis=1).reshape(features, extent)  36.6 us
    gather x64, local copies, waits for them, and re-layouts, allocate(): charged = jnp.take(prices, chosen, axis=0).reshape(extent)  35.6 us
    scatter-add x48, other arithmetic, advance(): outlay.at[chosen].add(jnp.sum(shares, axis=0).reshape(slot_count, BLOCK))  29.9 us
  transfers between devices with their start and end apart: 5, of which 4 were waited for; matrix products, arithmetic and copies ran while one was open for 0% of the time, Pallas kernels for 0%

profile of v1, /device:TPU:25, one launch (start us, length us, event | category | flops | bytes accessed | tf_op | source)
XLA Modules:
  0.0 1107.5 jit_solution(7616647094819972915)
XLA Ops:
  9.4 44.2 %all_gather.3 = bf16[64,4096]{1,0:T(8,128)(2,1)S(1)} all-gather(bf16[64,128]{1,0:T(8,128)(2,1)S(1)} %copy-done.7), channel_id=1, replica_groups=mesh['imp'=32,'adv'=16] {'imp'}, dimensions={1}, use_global_device_ids=true | all-gather | bytes 540672 | tf_op jit(solution)/shard_map/all_gather | solution.py:23
  53.8 41.5 %while.60 = (s32[]{:T(128)}, f32[32,128]{1,0:T(8,128)S(1)}, f32[2048]{0:T(1024)S(1)}, s32[16,8]{1,0:T(8,128)S(1)}, bf16[64,16,128]{2,0,1:T(8,128)(2,1)S(1)}, /*i...) while((s32[]{:T(128)}, f32[32,128]{1,0:T(8,128)S(1)}, ...), condition=%wide.region_4.7_spmd, body=%wide.region_0.6_spmd.sunk | while | flops 17500104 | bytes 485907 | solution.py:61
  95.3 112.7 %all-reduce = f32[4096]{0:T(1024)S(1)} all-reduce(f32[4096]{0:T(1024)S(1)} %bitcast.252), channel_id=2, replica_groups=mesh['imp'=32,'adv'=16] {'imp'}, use_global_device_ids=true, to_apply=%region_5.8.clone | all-reduce | flops 4096 | bytes 32768
  208.0 1.3 dynamic-slice
  210.7 3.8 all-to-all-start
  214.5 64.0 %psum.21 = f32[2048]{0:T(1024)S(1)} all-reduce(f32[2048]{0:T(1024)S(1)} %get-tuple-element.597), channel_id=1, replica_groups=mesh['imp'=32,'adv'=16] {'adv'}, use_global_device_ids=true, to_apply=%region_6.9 | all-reduce | flops 2048 | bytes 16384 | tf_op jit(solution)/shard_map/psum | solution.py:64
  278.6 42.5 %while.61 = (s32[]{:T(128)}, f32[32,128]{1,0:T(8,128)S(1)}, f32[2048]{0:T(1024)S(1)}, s32[16,8]{1,0:T(8,128)S(1)}, bf16[64,16,128]{2,0,1:T(8,128)(2,1)S(1)}, /*i...) while((s32[]{:T(128)}, f32[32,128]{1,0:T(8,128)S(1)}, ...), condition=%wide.region_11.14_spmd, body=%wide.region_7.13_spmd.sunk | while | flops 17631180 | bytes 471067 | solution.py:61
  321.1 24.1 %psum.22 = f32[2048]{0:T(1024)S(1)} all-reduce(f32[2048]{0:T(1024)S(1)} %get-tuple-element.599), channel_id=1, replica_groups=mesh['imp'=32,'adv'=16] {'adv'}, use_global_device_ids=true, to_apply=%region_13.16 | all-reduce | flops 2048 | bytes 16384 | tf_op jit(solution)/shard_map/psum | solution.py:64
  345.2 115.0 %all-reduce.1 = f32[4096]{0:T(1024)S(1)} all-reduce(f32[4096]{0:T(1024)S(1)} %bitcast.253), channel_id=3, replica_groups=mesh['imp'=32,'adv'=16] {'imp'}, use_global_device_ids=true, to_apply=%region_12.15.clone | all-reduce | flops 4096 | bytes 32768
  460.8 4.4 all-to-all-start.1
  465.3 8.5 all-to-all-done.1
  473.8 42.5 %while.62 = (s32[]{:T(128)}, f32[32,128]{1,0:T(8,128)S(1)}, f32[2048]{0:T(1024)S(1)}, s32[16,8]{1,0:T(8,128)S(1)}, bf16[64,16,128]{2,0,1:T(8,128)(2,1)S(1)}, /*i...) while((s32[]{:T(128)}, f32[32,128]{1,0:T(8,128)S(1)}, ...), condition=%wide.region_18.21_spmd, body=%wide.region_14.20_spmd.sunk | while | flops 17631180 | bytes 471067 | solution.py:61
  516.3 53.3 %psum.23 = f32[2048]{0:T(1024)S(1)} all-reduce(f32[2048]{0:T(1024)S(1)} %get-tuple-element.601), channel_id=1, replica_groups=mesh['imp'=32,'adv'=16] {'adv'}, use_global_device_ids=true, to_apply=%region_20.23 | all-reduce | flops 2048 | bytes 16384 | tf_op jit(solution)/shard_map/psum | solution.py:64
  569.6 111.1 %all-reduce.2 = f32[4096]{0:T(1024)S(1)} all-reduce(f32[4096]{0:T(1024)S(1)} %bitcast.254), channel_id=4, replica_groups=mesh['imp'=32,'adv'=16] {'imp'}, use_global_device_ids=true, to_apply=%region_19.22.clone | all-reduce | flops 4096 | bytes 32768
  681.4 4.2 all-to-all-start.2
  686.2 7.9 all-to-all-done.2
  694.3 95.1 %while.63 = (s32[]{:T(128)}, f32[64,2048]{1,0:T(8,128)S(1)}, f32[64,32,128]{2,0,1:T(8,128)S(1)}, s32[16,8]{1,0:T(8,128)S(1)}, bf16[64,32,128]{2,0,1:T(8,128)(2,1...) while((s32[]{:T(128)}, f32[64,2048]{1,0:T(8,128)S(1)}, ...), condition=%wide.region_23.26_spmd, body=%wide.region_21.25_spmd.sunk | while | flops 51185740 | bytes 2993603 | solution.py:89
  699.3 0.9 scatter_fusion
  705.2 0.9 scatter_fusion
  790.2 1.3 copy.68
  792.3 240.9 %reduce-scatter.7.cloned.1.call-done = bf16[128,64]{1,0:T(8,128)(2,1)} async-done(((bf16[4096,64]{1,0:T(8,128)(2,1)}), bf16[128,64]{1,0:T(8,128)(2,1)}) %reduce-scatter.7.cloned.1.call-update) | async-done | bytes 16400
  1033.3 1.4 copy.67
  1034.7 64.6 %reduce-scatter.5.cloned.1.call-done = f32[64,128]{1,0:T(8,128)} async-done(((f32[64,2048]{1,0:T(8,128)}), f32[64,128]{1,0:T(8,128)}) %reduce-scatter.5.cloned.1.call-update) | async-done | bytes 32784 | tf_op jit(solution)/shard_map/reduce_scatter | solution.py:90
  1099.3 1.4 convert_element_type.23
  (1002 shorter events, 221.5 us)
Async XLA Ops:
  7.2 1.6 copy-start
  210.7 67.9 %all-to-all-start = ((f32[32,1,128]{2,1,0:T(1,128)}), f32[32,1,128]{2,1,0:T(1,128)S(1)}, u32[]{:S(2)}, u32[]{:S(2)}) async-start(f32[32,1,128]{2,1,0:T(1,128)} %stack.6), calls=%async_computation | async-start | bytes 32768 | tf_op jit(solution)/shard_map/all_to_all | solution.py:68
  214.5 64.1 %copy-start.2 = (f32[2048]{0:T(1024)S(1)}, f32[2048]{0:T(1024)}, u32[]{:S(2)}) copy-start(f32[2048]{0:T(1024)} %param.21) | copy-start | bytes 24580
  460.8 12.9 %all-to-all-start.1 = ((f32[32,1,128]{2,1,0:T(1,128)}), f32[32,1,128]{2,1,0:T(1,128)S(1)}, u32[]{:S(2)}, u32[]{:S(2)}) async-start(f32[32,1,128]{2,1,0:T(1,128)} %stack.7), calls=%async_computation.1 | async-start | bytes 32768 | tf_op jit(solution)/shard_map/all_to_all | solution.py:68
  681.4 12.7 %all-to-all-start.2 = ((f32[32,1,128]{2,1,0:T(1,128)}), f32[32,1,128]{2,1,0:T(1,128)S(1)}, u32[]{:S(2)}, u32[]{:S(2)}) async-start(f32[32,1,128]{2,1,0:T(1,128)} %stack.8), calls=%async_computation.2 | async-start | bytes 32768 | tf_op jit(solution)/shard_map/all_to_all | solution.py:68
  685.6 347.7 %reduce-scatter.7.cloned.1.call-start = ((), (), s32[]{:S(2)}) async-start(), calls=%async_computation.6 | async-start | bytes 1081344
  694.3 2.0 copy-start.5
  696.3 1.2 copy-start.3
  700.2 2.0 copy-start.5
  706.2 2.0 copy-start.5
  712.1 2.0 copy-start.5
  718.1 2.0 copy-start.5
  724.0 2.0 copy-start.5
  730.0 2.0 copy-start.5
  735.9 2.0 copy-start.5
  741.9 2.0 copy-start.5
  747.8 2.0 copy-start.5
  753.7 2.0 copy-start.5
  759.7 2.0 copy-start.5
  765.6 2.0 copy-start.5
  771.6 2.0 copy-start.5
  777.5 2.0 copy-start.5
  783.5 2.0 copy-start.5
  791.6 307.7 %reduce-scatter.5.cloned.1.call-start = ((), (), s32[]{:S(2)}) async-start(), calls=%async_computation.5 | async-start | bytes 557056 | tf_op jit(solution)/shard_map/reduce_scatter | solution.py:90
  (101 other events, 82.3 us)
Sparse Core Ops, SparseCore 0:
  791.7 241.5 reduce-scatter.6
  1036.0 63.1 reduce-scatter.4
